TPU v7x, 32 devices: a whole 2x2x4 slice. The times are simulated.
32 devices in a mesh: sect: 4 (over x, core), batch: 8 (over z, y).
Axes of the slice: x: 2, y: 2, z: 4, core: 2. Of those that a mesh axis runs over, the one named last changes fastest.
Arguments:
- warm: bfloat16 [8192, 640], P(('sect', 'batch')), may hold values from -6 to 6
- latents: float32 [4, 1024], P(None, 'batch'), may hold values from -6 to 6
- timesteps: int32 [5], replicated, may hold values from 300 to 599
- assign: int32 [8], P('batch'), may hold values from 0 to 7, each once
- prompts: bfloat16 [8, 640], P('batch'), may hold values from -6 to 6
- w_in: bfloat16 [2560, 2560], P('sect'), may hold values from -0.25 to 0.25
- time_w: bfloat16 [2560, 640], P('sect'), may hold values from -0.25 to 0.25
- w_out: bfloat16 [5120, 640], P(('sect', 'batch')), may hold values from -0.15625 to 0.15625
- conv_in_w: bfloat16 [4, 640], replicated, may hold values from -3 to 3
- conv_out_w: bfloat16 [4, 640], replicated, may hold values from -0.25 to 0.25
Outputs:
- segments: bfloat16 [8192, 640], P(('sect', 'batch'))
- final_latents: float32 [4, 1024], P('sect', 'batch')
Inputs may be any that keep to these rules, and one draw needn't show every extreme that they name: `assign`: each prompt is assigned to exactly one prompt batch.
All inputs are finite; a program needn't handle non-finite values.
Results may differ from a plain program's by a relative error of at most 0.015.
Values may be sent and summed in bfloat16 or wider, within the bound.
A program may use at most 64 MiB of HBM per device.

v0:
```python
import math
import jax
import jax.numpy as jnp
from jax import lax
from jax.sharding import PartitionSpec as P

guidance_scale = 3.0


def passed_along(shard, axis, by):
    devices = lax.axis_size(axis)
    pairs = [(i, i + by) for i in range(devices) if 0 <= i + by < devices]
    return lax.ppermute(shard, axis, pairs)


def from_behind(block, axis, distance):
    devices = range(lax.axis_size(axis))
    route = [((i - distance) % len(devices), i) for i in devices]
    return lax.ppermute(block, axis, route)


def broadcast(block, axis, source):
    block = jnp.where(lax.axis_index(axis) == source, block, jnp.zeros_like(block))
    return lax.psum(block, axis)


def sinusoid(time_value, channels):
    half_width = channels // 2
    frequency = jnp.exp(-math.log(10000.0) * jnp.arange(half_width, dtype=jnp.float32) / half_width)
    angles = time_value.astype(jnp.float32) * frequency
    return jnp.concatenate([jnp.cos(angles), jnp.sin(angles)])


def alpha_bar(time_value):
    phase_angle = (time_value.astype(jnp.float32) / 1000.0 + 0.008) / 1.008 * (math.pi / 2)
    return jnp.cos(phase_angle) ** 2


def rms_norm(values):
    return values * lax.rsqrt(jnp.mean(values * values, axis=-1, keepdims=True) + 1e-06)


def feed_block(inputs, time_vec, cond_rows, weight_in, weight_out, hidden_units):
    summed = inputs + time_vec + cond_rows
    normed = rms_norm(summed).astype(jnp.bfloat16)
    projected = jnp.dot(normed, weight_in, preferred_element_type=jnp.float32)
    hidden = (
        projected[:, :hidden_units] * jax.nn.gelu(projected[:, hidden_units:], approximate=False)
    ).astype(jnp.bfloat16)
    return (summed + jnp.dot(hidden, weight_out, preferred_element_type=jnp.float32)).astype(
        jnp.bfloat16
    )


def on_device(
    warm, latents, timesteps, assign, prompts, w_in, time_w, w_out, conv_in_w, conv_out_w
):
    section = lax.axis_index("sect")
    sect_count = lax.axis_size("sect")
    last_index = sect_count - 1
    w_out_all, table = (
        lax.all_gather(w_out, "batch", axis=0, tiled=True),
        lax.all_gather(prompts, "batch", axis=0, tiled=True),
    )
    positions = latents.shape[1]
    channels = warm.shape[1]
    hidden_units = w_out_all.shape[0]
    picker = (jnp.arange(table.shape[0], dtype=jnp.int32)[None, :] == assign[:, None]).astype(
        jnp.bfloat16
    )
    chosen = jnp.dot(picker, table, preferred_element_type=jnp.float32)
    cond = jnp.concatenate(
        [
            jnp.broadcast_to(chosen, (positions, channels)),
            jnp.zeros((positions, channels), jnp.float32),
        ],
        axis=0,
    )
    segment = warm
    latent = latents
    for step_index in range(timesteps.shape[0] - 1):
        time_now = timesteps[step_index]
        time_next = timesteps[step_index + 1]
        received = passed_along(segment, "sect", 1)
        skipped = from_behind(segment, "sect", -1)
        embedded = jax.nn.silu(sinusoid(time_now, channels)).astype(jnp.bfloat16)
        first = lax.dot_general(
            latent.astype(jnp.bfloat16),
            conv_in_w,
            (((0,), (0,)), ((), ())),
            preferred_element_type=jnp.float32,
        ).astype(jnp.bfloat16)
        first = jnp.concatenate([first, first], axis=0)
        inputs = jnp.where(section == 0, first, received).astype(jnp.float32)
        inputs = (inputs + skipped.astype(jnp.float32)) * 0.5
        time_vec = jnp.dot(embedded[None, :], time_w, preferred_element_type=jnp.float32)
        segment = feed_block(inputs, time_vec, cond, w_in, w_out_all, hidden_units)
        activated = jax.nn.silu(rms_norm(segment.astype(jnp.float32))).astype(jnp.bfloat16)
        noise = lax.dot_general(
            conv_out_w, activated, (((1,), (1,)), ((), ())), preferred_element_type=jnp.float32
        )
        guided = noise[:, positions:] + guidance_scale * (
            noise[:, :positions] - noise[:, positions:]
        )
        bar_now = alpha_bar(time_now)
        bar_next = alpha_bar(time_next)
        clean = (latent - jnp.sqrt(1.0 - bar_now) * guided) / jnp.sqrt(bar_now)
        updated = jnp.sqrt(bar_next) * clean + jnp.sqrt(1.0 - bar_next) * guided
        latent = broadcast(updated, "sect", last_index)
    channels_here = latent.shape[0] // sect_count
    own_latent = lax.dynamic_slice_in_dim(latent, section * channels_here, channels_here, 0)
    return (segment, own_latent)


def solution(mesh):
    return jax.shard_map(
        on_device,
        mesh=mesh,
        in_specs=(
            P(("sect", "batch"), None),
            P(None, "batch"),
            P(),
            P("batch"),
            P("batch", None),
            P("sect", None),
            P("sect", None),
            P(("sect", "batch"), None),
            P(),
            P(),
        ),
        out_specs=(P(("sect", "batch"), None), P("sect", "batch")),
        check_vma=False,
    )
```

profile of v0, /device:TPU:0, one launch (start us, length us, event | category | flops | bytes accessed | tf_op | source)
XLA Modules:
  0.0 147.3 jit_solution(3572738905589902597)
XLA Ops:
  7.9 3.2 %collective-permute-start = (bf16[256,640]{1,0:T(8,128)(2,1)}, bf16[256,640]{1,0:T(8,128)(2,1)}, u32[]{:S(2)}, u32[]{:S(2)}) collective-permute-start(bf16[256,640]{1,0:T(8,128)(2,1)} %param.10), channel_id=1, source_target_pairs={{0,8},{8,16},{16,24},{1,9},{9,17},{17,25},{2,10},{10,18},{18,26},{... | collective-permute-start | bytes 983048 | tf_op jit(solution)/shard_map/ppermute | solution.py:13
  11.8 1.5 %fusion.362 = (s32[1]{0:T(128)}, s32[1]{0:T(128)}, s32[1]{0:T(128)}, s32[1]{0:T(128)}, s32[1]{0:T(128)}) fusion(s32[5]{0:T(128)} %param.12), kind=kLoop, calls=%fused_computation.457 | loop fusion | bytes 40 | tf_op jit(solution)/shard_map/slice | solution.py:83
  18.7 31.3 %all-gather = bf16[8,1,640]{2,1,0:T(2,128)(2,1)S(1)} all-gather(bf16[1,1,640]{2,1,0:T(2,128)(2,1)} %bitcast.47), channel_id=1, replica_groups=mesh['sect'=4,'batch'=8] {'batch'}, dimensions={0}, use_global_device_ids=true | all-gather | bytes 11520 | tf_op jit(solution)/shard_map/all_gather | solution.py:63
  50.0 1.4 convolution_reduce_fusion.4
  51.4 1.4 convolution_reduce_fusion.3
  53.8 1.4 multiply_reduce_fusion.3
  55.2 3.8 %fusion.196 = f32[256,2560]{1,0:T(8,128)} fusion(bf16[640,2560]{1,0:T(8,128)(2,1)S(1)} %copy-done, f32[256]{0:T(256)S(1)} %add_rsqrt_fusion.7, f32[128,640]{1,0:T(8,128)S(1)} %broadcast_in_dim.2, bf16[256,640]{1,0:T(8,128)(2,1)} %collective-permute-done.1, bf16[256,640]{1,0:T(8,128)(2,1)} %collective-permute-done, ...), kind=kOutput, calls=%fused_computation.265 | convolution fusion | flops 840990720 | bytes 7048705 | tf_op jit(solution)/shard_map/dot_general | solution.py:46
  59.0 6.4 %fusion.72 = (f32[256]{0:T(256)S(1)}, bf16[256,640]{1,0:T(8,128)(2,1)}) fusion(bf16[1280,640]{1,0:T(8,128)(2,1)} %all-gather.3.cloned.1.call-done, f32[256,2560]{1,0:T(8,128)} %fusion.196, f32[128,640]{1,0:T(8,128)} %copy-done.1, f32[640]{0:T(1024)S(1)} %convolution_reduce_fusion.4, bf16[256,640]{1,0:T(8,128)(2,1)} %collective-permute-done.1, ...), kind=kOutput, calls=%fused_computation.137 | convolution fusion | flops 443678464 | bytes 5737985 | tf_op jit(solution)/shard_map/dot_general | solution.py:50
  65.4 2.0 %collective-permute-start.2 = (bf16[256,640]{1,0:T(8,128)(2,1)}, bf16[256,640]{1,0:T(8,128)(2,1)}, u32[]{:S(2)}, u32[]{:S(2)}) collective-permute-start(bf16[256,640]{1,0:T(8,128)(2,1)} %get-tuple-element.8), channel_id=1, source_target_pairs={{0,8},{8,16},{16,24},{1,9},{9,17},{17,25},{2,10},{10,18},{18,26},{... | collective-permute-start | bytes 983048 | tf_op jit(solution)/shard_map/ppermute | solution.py:13
  68.8 9.1 %psum.28 = f32[4,128]{1,0:T(4,128)S(1)} all-reduce(f32[4,128]{1,0:T(4,128)S(1)} %add_select_fusion.3), channel_id=1, replica_groups=mesh['sect'=4,'batch'=8] {'sect'}, use_global_device_ids=true, to_apply=%region_2.3 | all-reduce | flops 512 | bytes 4096 | tf_op jit(solution)/shard_map/psum | solution.py:24
  78.2 1.4 multiply_reduce_fusion.2
  79.6 2.4 %fusion.197 = f32[256,2560]{1,0:T(8,128)S(1)} fusion(bf16[640,2560]{1,0:T(8,128)(2,1)S(1)} %copy-done, f32[256]{0:T(256)S(1)} %add_rsqrt_fusion.5, f32[128,640]{1,0:T(8,128)S(1)} %copy-done.2, bf16[256,640]{1,0:T(8,128)(2,1)} %collective-permute-done.3, bf16[256,640]{1,0:T(8,128)(2,1)} %collective-permute-done.2, ...), kind=kOutput, calls=%fused_computation.266 | convolution fusion | flops 840990720 | bytes 7048705 | tf_op jit(solution)/shard_map/dot_general | solution.py:46
  82.0 5.2 %fusion.73 = (f32[256]{0:T(256)S(1)}, bf16[256,640]{1,0:T(8,128)(2,1)}) fusion(bf16[1280,640]{1,0:T(8,128)(2,1)S(1)} %copy-done.8, f32[256,2560]{1,0:T(8,128)S(1)} %fusion.197, f32[128,640]{1,0:T(8,128)S(1)} %copy-done.2, f32[640]{0:T(1024)S(1)} %convolution_reduce_fusion.3, bf16[256,640]{1,0:T(8,128)(2,1)} %collective-permute-done.3, ...), kind=kOutput, calls=%fused_computation.138 | convolution fusion | flops 443678464 | bytes 5737985 | tf_op jit(solution)/shard_map/dot_general | solution.py:50
  87.2 3.0 %collective-permute-start.4 = (bf16[256,640]{1,0:T(8,128)(2,1)}, bf16[256,640]{1,0:T(8,128)(2,1)}, u32[]{:S(2)}, u32[]{:S(2)}) collective-permute-start(bf16[256,640]{1,0:T(8,128)(2,1)} %get-tuple-element.10), channel_id=1, source_target_pairs={{0,8},{8,16},{16,24},{1,9},{9,17},{17,25},{2,10},{10,18},{18,26},{... | collective-permute-start | bytes 983048 | tf_op jit(solution)/shard_map/ppermute | solution.py:13
  91.6 9.8 %psum.29 = f32[4,128]{1,0:T(4,128)S(1)} all-reduce(f32[4,128]{1,0:T(4,128)S(1)} %add_select_fusion.2), channel_id=1, replica_groups=mesh['sect'=4,'batch'=8] {'sect'}, use_global_device_ids=true, to_apply=%region_5.6 | all-reduce | flops 512 | bytes 4096 | tf_op jit(solution)/shard_map/psum | solution.py:24
  101.6 1.4 multiply_reduce_fusion.1
  103.0 2.4 %fusion.198 = f32[256,2560]{1,0:T(8,128)S(1)} fusion(bf16[640,2560]{1,0:T(8,128)(2,1)S(1)} %copy-done, f32[256]{0:T(256)S(1)} %add_rsqrt_fusion.3, f32[128,640]{1,0:T(8,128)S(1)} %copy-done.3, bf16[256,640]{1,0:T(8,128)(2,1)} %collective-permute-done.5, bf16[256,640]{1,0:T(8,128)(2,1)} %collective-permute-done.4, ...), kind=kOutput, calls=%fused_computation.267 | convolution fusion | flops 840990720 | bytes 7048705 | tf_op jit(solution)/shard_map/dot_general | solution.py:46
  105.4 5.2 %fusion.74 = (f32[256]{0:T(256)S(1)}, bf16[256,640]{1,0:T(8,128)(2,1)}) fusion(bf16[1280,640]{1,0:T(8,128)(2,1)S(1)} %copy-done.9, f32[256,2560]{1,0:T(8,128)S(1)} %fusion.198, f32[128,640]{1,0:T(8,128)S(1)} %copy-done.3, f32[640]{0:T(1024)S(1)} %convolution_reduce_fusion.2, bf16[256,640]{1,0:T(8,128)(2,1)} %collective-permute-done.5, ...), kind=kOutput, calls=%fused_computation.139 | convolution fusion | flops 443678464 | bytes 5737985 | tf_op jit(solution)/shard_map/dot_general | solution.py:50
  110.6 2.0 %collective-permute-start.6 = (bf16[256,640]{1,0:T(8,128)(2,1)}, bf16[256,640]{1,0:T(8,128)(2,1)}, u32[]{:S(2)}, u32[]{:S(2)}) collective-permute-start(bf16[256,640]{1,0:T(8,128)(2,1)} %get-tuple-element.12), channel_id=1, source_target_pairs={{0,8},{8,16},{16,24},{1,9},{9,17},{17,25},{2,10},{10,18},{18,26},{... | collective-permute-start | bytes 983048 | tf_op jit(solution)/shard_map/ppermute | solution.py:13
  114.2 10.5 %psum.30 = f32[4,128]{1,0:T(4,128)S(1)} all-reduce(f32[4,128]{1,0:T(4,128)S(1)} %add_select_fusion.1), channel_id=1, replica_groups=mesh['sect'=4,'batch'=8] {'sect'}, use_global_device_ids=true, to_apply=%region_8.9 | all-reduce | flops 512 | bytes 4096 | tf_op jit(solution)/shard_map/psum | solution.py:24
  125.0 1.4 multiply_reduce_fusion
  126.4 2.4 %fusion.199 = f32[256,2560]{1,0:T(8,128)S(1)} fusion(bf16[640,2560]{1,0:T(8,128)(2,1)S(1)} %copy-done, f32[256]{0:T(256)S(1)} %add_rsqrt_fusion.1, f32[128,640]{1,0:T(8,128)S(1)} %copy-done.4, bf16[256,640]{1,0:T(8,128)(2,1)} %collective-permute-done.7, bf16[256,640]{1,0:T(8,128)(2,1)} %collective-permute-done.6, ...), kind=kOutput, calls=%fused_computation.268 | convolution fusion | flops 840990720 | bytes 7048705 | tf_op jit(solution)/shard_map/dot_general | solution.py:46
  128.8 4.6 %fusion.75 = (f32[256]{0:T(256)S(1)}, bf16[256,640]{1,0:T(8,128)(2,1)S(1)}) fusion(bf16[1280,640]{1,0:T(8,128)(2,1)S(1)} %copy-done.10, f32[256,2560]{1,0:T(8,128)S(1)} %fusion.199, f32[128,640]{1,0:T(8,128)S(1)} %copy-done.4, f32[640]{0:T(1024)S(1)} %convolution_reduce_fusion.1, bf16[256,640]{1,0:T(8,128)(2,1)} %collective-permute-done.7, ...), kind=kOutput, calls=%fused_computation.140 | convolution fusion | flops 443678464 | bytes 5737985 | tf_op jit(solution)/shard_map/dot_general | solution.py:50
  134.2 5.8 %psum.31 = f32[4,128]{1,0:T(4,128)S(1)} all-reduce(f32[4,128]{1,0:T(4,128)S(1)} %add_select_fusion), channel_id=1, replica_groups=mesh['sect'=4,'batch'=8] {'sect'}, use_global_device_ids=true, to_apply=%region_11.12 | all-reduce | flops 512 | bytes 4096 | tf_op jit(solution)/shard_map/psum | solution.py:24
  (78 shorter events, 9.3 us)
Async XLA Ops:
  7.2 48.0 %copy-start = (bf16[640,2560]{1,0:T(8,128)(2,1)S(1)}, bf16[640,2560]{1,0:T(8,128)(2,1)}, u32[]{:S(2)}) copy-start(bf16[640,2560]{1,0:T(8,128)(2,1)} %param.15) | copy-start | bytes 9830404
  7.2 51.8 %all-gather.3.cloned.1.call-start = ((), (), s32[]{:S(2)}) async-start(), calls=%async_computation | async-start | bytes 1843200 | tf_op jit(solution)/shard_map/all_gather | solution.py:62
  7.9 45.8 %collective-permute-start = (bf16[256,640]{1,0:T(8,128)(2,1)}, bf16[256,640]{1,0:T(8,128)(2,1)}, u32[]{:S(2)}, u32[]{:S(2)}) collective-permute-start(bf16[256,640]{1,0:T(8,128)(2,1)} %param.10), channel_id=1, source_target_pairs={{0,8},{8,16},{16,24},{1,9},{9,17},{17,25},{2,10},{10,18},{18,26},{... | collective-permute-start | bytes 983048 | tf_op jit(solution)/shard_map/ppermute | solution.py:13
  11.1 42.6 %collective-permute-start.1 = (bf16[256,640]{1,0:T(8,128)(2,1)}, bf16[256,640]{1,0:T(8,128)(2,1)}, u32[]{:S(2)}, u32[]{:S(2)}) collective-permute-start(bf16[256,640]{1,0:T(8,128)(2,1)} %param.10), channel_id=1, source_target_pairs={{8,0},{16,8},{24,16},{0,24},{9,1},{17,9},{25,17},{1,25},{10,2},{18... | collective-permute-start | bytes 983048 | tf_op jit(solution)/shard_map/ppermute | solution.py:19
  18.7 34.1 %copy-start.5 = (bf16[640,640]{1,0:T(8,128)(2,1)S(1)}, bf16[640,640]{1,0:T(8,128)(2,1)}, u32[]{:S(2)}) copy-start(bf16[640,640]{1,0:T(8,128)(2,1)} %param.16) | copy-start | bytes 2457604
  51.4 2.1 %copy-start.6 = (bf16[4,640]{1,0:T(4,128)(2,1)S(1)}, bf16[4,640]{1,0:T(4,128)(2,1)}, u32[]{:S(2)}) copy-start(bf16[4,640]{1,0:T(4,128)(2,1)} %param.18) | copy-start | bytes 15364
  51.4 2.1 %copy-start.7 = (f32[4,128]{1,0:T(4,128)S(1)}, f32[4,128]{1,0:T(4,128)}, u32[]{:S(2)}) copy-start(f32[4,128]{1,0:T(4,128)} %param.11) | copy-start | bytes 6148
  53.8 1.4 copy-start.1
  59.0 8.4 %copy-start.11 = (bf16[4,640]{1,0:T(4,128)(2,1)S(1)}, bf16[4,640]{1,0:T(4,128)(2,1)}, u32[]{:S(2)}) copy-start(bf16[4,640]{1,0:T(4,128)(2,1)} %param.19) | copy-start | bytes 15364
  65.4 12.8 %collective-permute-start.2 = (bf16[256,640]{1,0:T(8,128)(2,1)}, bf16[256,640]{1,0:T(8,128)(2,1)}, u32[]{:S(2)}, u32[]{:S(2)}) collective-permute-start(bf16[256,640]{1,0:T(8,128)(2,1)} %get-tuple-element.8), channel_id=1, source_target_pairs={{0,8},{8,16},{16,24},{1,9},{9,17},{17,25},{2,10},{10,18},{18,26},{... | collective-permute-start | bytes 983048 | tf_op jit(solution)/shard_map/ppermute | solution.py:13
  67.4 10.8 %collective-permute-start.3 = (bf16[256,640]{1,0:T(8,128)(2,1)}, bf16[256,640]{1,0:T(8,128)(2,1)}, u32[]{:S(2)}, u32[]{:S(2)}) collective-permute-start(bf16[256,640]{1,0:T(8,128)(2,1)} %get-tuple-element.8), channel_id=1, source_target_pairs={{8,0},{16,8},{24,16},{0,24},{9,1},{17,9},{25,17},{1,25},{10,2},{18... | collective-permute-start | bytes 983048 | tf_op jit(solution)/shard_map/ppermute | solution.py:19
  78.0 1.6 %copy-start.2 = (f32[128,640]{1,0:T(8,128)S(1)}, f32[128,640]{1,0:T(8,128)}, u32[]{:S(2)}) copy-start(f32[128,640]{1,0:T(8,128)} %copy-done.1) | copy-start | bytes 983044
  79.6 2.4 %copy-start.8 = (bf16[1280,640]{1,0:T(8,128)(2,1)S(1)}, bf16[1280,640]{1,0:T(8,128)(2,1)}, u32[]{:S(2)}) copy-start(bf16[1280,640]{1,0:T(8,128)(2,1)} %all-gather.3.cloned.1.call-done) | copy-start | bytes 4915204
  87.2 14.4 %collective-permute-start.4 = (bf16[256,640]{1,0:T(8,128)(2,1)}, bf16[256,640]{1,0:T(8,128)(2,1)}, u32[]{:S(2)}, u32[]{:S(2)}) collective-permute-start(bf16[256,640]{1,0:T(8,128)(2,1)} %get-tuple-element.10), channel_id=1, source_target_pairs={{0,8},{8,16},{16,24},{1,9},{9,17},{17,25},{2,10},{10,18},{18,26},{... | collective-permute-start | bytes 983048 | tf_op jit(solution)/shard_map/ppermute | solution.py:13
  90.2 11.5 %collective-permute-start.5 = (bf16[256,640]{1,0:T(8,128)(2,1)}, bf16[256,640]{1,0:T(8,128)(2,1)}, u32[]{:S(2)}, u32[]{:S(2)}) collective-permute-start(bf16[256,640]{1,0:T(8,128)(2,1)} %get-tuple-element.10), channel_id=1, source_target_pairs={{8,0},{16,8},{24,16},{0,24},{9,1},{17,9},{25,17},{1,25},{10,2},{18... | collective-permute-start | bytes 983048 | tf_op jit(solution)/shard_map/ppermute | solution.py:19
  101.4 1.6 %copy-start.3 = (f32[128,640]{1,0:T(8,128)S(1)}, f32[128,640]{1,0:T(8,128)}, u32[]{:S(2)}) copy-start(f32[128,640]{1,0:T(8,128)} %copy-done.1) | copy-start | bytes 983044
  103.0 2.4 %copy-start.9 = (bf16[1280,640]{1,0:T(8,128)(2,1)S(1)}, bf16[1280,640]{1,0:T(8,128)(2,1)}, u32[]{:S(2)}) copy-start(bf16[1280,640]{1,0:T(8,128)(2,1)} %all-gather.3.cloned.1.call-done) | copy-start | bytes 4915204
  110.6 14.4 %collective-permute-start.6 = (bf16[256,640]{1,0:T(8,128)(2,1)}, bf16[256,640]{1,0:T(8,128)(2,1)}, u32[]{:S(2)}, u32[]{:S(2)}) collective-permute-start(bf16[256,640]{1,0:T(8,128)(2,1)} %get-tuple-element.12), channel_id=1, source_target_pairs={{0,8},{8,16},{16,24},{1,9},{9,17},{17,25},{2,10},{10,18},{18,26},{... | collective-permute-start | bytes 983048 | tf_op jit(solution)/shard_map/ppermute | solution.py:13
  112.6 12.4 %collective-permute-start.7 = (bf16[256,640]{1,0:T(8,128)(2,1)}, bf16[256,640]{1,0:T(8,128)(2,1)}, u32[]{:S(2)}, u32[]{:S(2)}) collective-permute-start(bf16[256,640]{1,0:T(8,128)(2,1)} %get-tuple-element.12), channel_id=1, source_target_pairs={{8,0},{16,8},{24,16},{0,24},{9,1},{17,9},{25,17},{1,25},{10,2},{18... | collective-permute-start | bytes 983048 | tf_op jit(solution)/shard_map/ppermute | solution.py:19
  124.7 1.6 %copy-start.4 = (f32[128,640]{1,0:T(8,128)S(1)}, f32[128,640]{1,0:T(8,128)}, u32[]{:S(2)}) copy-start(f32[128,640]{1,0:T(8,128)} %copy-done.1) | copy-start | bytes 983044
  126.4 2.4 %copy-start.10 = (bf16[1280,640]{1,0:T(8,128)(2,1)S(1)}, bf16[1280,640]{1,0:T(8,128)(2,1)}, u32[]{:S(2)}) copy-start(bf16[1280,640]{1,0:T(8,128)(2,1)} %all-gather.3.cloned.1.call-done) | copy-start | bytes 4915204
  133.4 0.7 copy-start.12
Sparse Core Ops, SparseCore 0:
  10.2 47.5 all-gather.2
where the time goes:
time: 148 us; the launch traced here: 147 us
  blocking collectives  66.5 us (45%)
  matrix products  41 us (28%)
  between operations  19.2 us (13%)
  starting transfers between devices  11.1 us (8%)
  other arithmetic  6.24 us (4%)
  local copies, waits for them, and re-layouts  2.51 us (2%)
    psum x4, blocking collectives, broadcast(): return lax.psum(block, axis)  35.2 us
    all_gather x1, blocking collectives, on_device(): lax.all_gather(prompts, 'batch', axis=0, tiled=True)  31.3 us
    dot_general x4, matrix products, feed_block(): jnp.dot(hidden, weight_out, preferred_element_type=jnp.float32)  21.4 us
    dot_general x4, matrix products, feed_block(): projected = jnp.dot(normed, weight_in, preferred_element_type=jnp.float32)  11 us
    ppermute x4, starting transfers between devices, passed_along(): return lax.ppermute(shard, axis, pairs)  10.2 us
    reduce_sum x4, other arithmetic, rms_norm(): jnp.mean(values * values, axis=-1, keepdims=True) + 1e-06  5.44 us
    dot_general x4, matrix products, on_device(): lax.dot_general(conv_out_w, activated, (((1,), (1,)), ((), ())), preferre...  4.33 us
    dot_general x4, matrix products, on_device(): jnp.dot(embedded[None, :], time_w, preferred_element_type=jnp.float32)  3.26 us
  transfers between devices with their start and end apart: 9, of which 0 were waited for; matrix products, arithmetic and copies ran while one was open for 11% of the time, Pallas kernels for 0%

commit v1 on v0

--- a/solution.py
+++ b/solution.py
@@ -21,7 +21,8 @@
 
 def broadcast(block, axis, source):
     block = jnp.where(lax.axis_index(axis) == source, block, jnp.zeros_like(block))
-    return lax.psum(block, axis)
+    _change_cards = lambda z_in, link_axis: jnp.sum(lax.all_gather(z_in, link_axis), axis=0)
+    return _change_cards(block, axis)
 
 
 def sinusoid(time_value, channels):

time: 148 us -> 145 us (0.980)
  blocking collectives: 66.5 us -> 61.2 us
  starting transfers between devices: 11.1 us -> 13.7 us
    psum x4 -> x0, blocking collectives: 35.2 us -> none  [broadcast(): return lax.psum(block, axis)]
    all_gather x0 -> x4, blocking collectives: none -> 29.9 us  [broadcast(): lax.all_gather(z_in, link_axis)]
where the time goes in v1:
time: 145 us
  blocking collectives  61.2 us (42%)
  matrix products  41.1 us (28%)
  between operations  19.2 us (13%)
  starting transfers between devices  13.7 us (9%)
  other arithmetic  6.29 us (4%)
  local copies, waits for them, and re-layouts  2.51 us (2%)
    all_gather x1, blocking collectives, on_device(): lax.all_gather(prompts, 'batch', axis=0, tiled=True)  31.3 us
    all_gather x4, blocking collectives, broadcast(): lax.all_gather(z_in, link_axis)  29.9 us
    dot_general x4, matrix products, feed_block(): jnp.dot(hidden, weight_out, preferred_element_type=jnp.float32)  21.4 us
    ppermute x4, starting transfers between devices, passed_along(): return lax.ppermute(shard, axis, pairs)  11.6 us
    dot_general x4, matrix products, feed_block(): projected = jnp.dot(normed, weight_in, preferred_element_type=jnp.float32)  11 us
    reduce_sum x4, other arithmetic, rms_norm(): jnp.mean(values * values, axis=-1, keepdims=True) + 1e-06  5.43 us
    dot_general x4, matrix products, on_device(): lax.dot_general(conv_out_w, activated, (((1,), (1,)), ((), ())), preferre...  4.33 us
    dot_general x4, matrix products, on_device(): jnp.dot(embedded[None, :], time_w, preferred_element_type=jnp.float32)  3.26 us
  transfers between devices with their start and end apart: 9, of which 0 were waited for; matrix products, arithmetic and copies ran while one was open for 11% of the time, Pallas kernels for 0%

profile of v1, /device:TPU:0, one launch (start us, length us, event | category | flops | bytes accessed | tf_op | source)
XLA Modules:
  0.0 144.7 jit_solution(18309617896258268942)
XLA Ops:
  7.9 3.2 %collective-permute-start = (bf16[256,640]{1,0:T(8,128)(2,1)}, bf16[256,640]{1,0:T(8,128)(2,1)}, u32[]{:S(2)}, u32[]{:S(2)}) collective-permute-start(bf16[256,640]{1,0:T(8,128)(2,1)} %param.10), channel_id=1, source_target_pairs={{0,8},{8,16},{16,24},{1,9},{9,17},{17,25},{2,10},{10,18},{18,26},{... | collective-permute-start | bytes 983048 | tf_op jit(solution)/shard_map/ppermute | solution.py:13
  11.8 1.5 %fusion.362 = (s32[1]{0:T(128)}, s32[1]{0:T(128)}, s32[1]{0:T(128)}, s32[1]{0:T(128)}, s32[1]{0:T(128)}) fusion(s32[5]{0:T(128)} %param.12), kind=kLoop, calls=%fused_computation.457 | loop fusion | bytes 40 | tf_op jit(solution)/shard_map/slice | solution.py:84
  18.7 31.3 %all-gather.4 = bf16[8,1,640]{2,1,0:T(2,128)(2,1)S(1)} all-gather(bf16[1,1,640]{2,1,0:T(2,128)(2,1)} %bitcast.55), channel_id=1, replica_groups=mesh['sect'=4,'batch'=8] {'batch'}, dimensions={0}, use_global_device_ids=true | all-gather | bytes 11520 | tf_op jit(solution)/shard_map/all_gather | solution.py:64
  50.0 1.4 convolution_reduce_fusion.4
  51.4 1.4 convolution_reduce_fusion.3
  53.8 1.4 multiply_reduce_fusion.3
  55.2 3.8 %fusion.196 = f32[256,2560]{1,0:T(8,128)} fusion(bf16[640,2560]{1,0:T(8,128)(2,1)S(1)} %copy-done, f32[256]{0:T(256)S(1)} %add_rsqrt_fusion.7, f32[128,640]{1,0:T(8,128)S(1)} %broadcast_in_dim.2, bf16[256,640]{1,0:T(8,128)(2,1)} %collective-permute-done.1, bf16[256,640]{1,0:T(8,128)(2,1)} %collective-permute-done, ...), kind=kOutput, calls=%fused_computation.265 | convolution fusion | flops 840990720 | bytes 7048705 | tf_op jit(solution)/shard_map/dot_general | solution.py:47
  59.0 6.4 %fusion.72 = (f32[256]{0:T(256)S(1)}, bf16[256,640]{1,0:T(8,128)(2,1)}) fusion(bf16[1280,640]{1,0:T(8,128)(2,1)} %all-gather.11.cloned.1.call-done, f32[256,2560]{1,0:T(8,128)} %fusion.196, f32[128,640]{1,0:T(8,128)} %copy-done.1, f32[640]{0:T(1024)S(1)} %convolution_reduce_fusion.4, bf16[256,640]{1,0:T(8,128)(2,1)} %collective-permute-done.1, ...), kind=kOutput, calls=%fused_computation.137 | convolution fusion | flops 443678464 | bytes 5737985 | tf_op jit(solution)/shard_map/dot_general | solution.py:51
  65.4 2.0 %collective-permute-start.2 = (bf16[256,640]{1,0:T(8,128)(2,1)}, bf16[256,640]{1,0:T(8,128)(2,1)}, u32[]{:S(2)}, u32[]{:S(2)}) collective-permute-start(bf16[256,640]{1,0:T(8,128)(2,1)} %get-tuple-element.8), channel_id=1, source_target_pairs={{0,8},{8,16},{16,24},{1,9},{9,17},{17,25},{2,10},{10,18},{18,26},{... | collective-permute-start | bytes 983048 | tf_op jit(solution)/shard_map/ppermute | solution.py:13
  68.8 9.4 %all-gather.5 = f32[4,4,128]{2,1,0:T(4,128)S(1)} all-gather(f32[1,4,128]{2,1,0:T(4,128)S(1)} %select_bitcast_fusion.3), channel_id=2, replica_groups=mesh['sect'=4,'batch'=8] {'sect'}, dimensions={0}, use_global_device_ids=true | all-gather | bytes 10240 | tf_op jit(solution)/shard_map/all_gather | solution.py:24
  78.5 1.4 multiply_reduce_fusion.2
  79.9 2.4 %fusion.197 = f32[256,2560]{1,0:T(8,128)S(1)} fusion(bf16[640,2560]{1,0:T(8,128)(2,1)S(1)} %copy-done, f32[256]{0:T(256)S(1)} %add_rsqrt_fusion.5, f32[128,640]{1,0:T(8,128)S(1)} %copy-done.2, bf16[256,640]{1,0:T(8,128)(2,1)} %collective-permute-done.3, bf16[256,640]{1,0:T(8,128)(2,1)} %collective-permute-done.2, ...), kind=kOutput, calls=%fused_computation.266 | convolution fusion | flops 840990720 | bytes 7048705 | tf_op jit(solution)/shard_map/dot_general | solution.py:47
  82.3 5.2 %fusion.73 = (f32[256]{0:T(256)S(1)}, bf16[256,640]{1,0:T(8,128)(2,1)}) fusion(bf16[1280,640]{1,0:T(8,128)(2,1)S(1)} %copy-done.8, f32[256,2560]{1,0:T(8,128)S(1)} %fusion.197, f32[128,640]{1,0:T(8,128)S(1)} %copy-done.2, f32[640]{0:T(1024)S(1)} %convolution_reduce_fusion.3, bf16[256,640]{1,0:T(8,128)(2,1)} %collective-permute-done.3, ...), kind=kOutput, calls=%fused_computation.138 | convolution fusion | flops 443678464 | bytes 5737985 | tf_op jit(solution)/shard_map/dot_general | solution.py:51
  87.5 3.2 %collective-permute-start.4 = (bf16[256,640]{1,0:T(8,128)(2,1)}, bf16[256,640]{1,0:T(8,128)(2,1)}, u32[]{:S(2)}, u32[]{:S(2)}) collective-permute-start(bf16[256,640]{1,0:T(8,128)(2,1)} %get-tuple-element.10), channel_id=1, source_target_pairs={{0,8},{8,16},{16,24},{1,9},{9,17},{17,25},{2,10},{10,18},{18,26},{... | collective-permute-start | bytes 983048 | tf_op jit(solution)/shard_map/ppermute | solution.py:13
  92.1 6.5 %all-gather.6 = f32[4,4,128]{2,1,0:T(4,128)S(1)} all-gather(f32[1,4,128]{2,1,0:T(4,128)S(1)} %select_bitcast_fusion.2), channel_id=3, replica_groups=mesh['sect'=4,'batch'=8] {'sect'}, dimensions={0}, use_global_device_ids=true | all-gather | bytes 10240 | tf_op jit(solution)/shard_map/all_gather | solution.py:24
  98.9 1.4 multiply_reduce_fusion.1
  100.3 2.4 %fusion.198 = f32[256,2560]{1,0:T(8,128)S(1)} fusion(bf16[640,2560]{1,0:T(8,128)(2,1)S(1)} %copy-done, f32[256]{0:T(256)S(1)} %add_rsqrt_fusion.3, f32[128,640]{1,0:T(8,128)S(1)} %copy-done.3, bf16[256,640]{1,0:T(8,128)(2,1)} %collective-permute-done.5, bf16[256,640]{1,0:T(8,128)(2,1)} %collective-permute-done.4, ...), kind=kOutput, calls=%fused_computation.267 | convolution fusion | flops 840990720 | bytes 7048705 | tf_op jit(solution)/shard_map/dot_general | solution.py:47
  102.7 5.2 %fusion.74 = (f32[256]{0:T(256)S(1)}, bf16[256,640]{1,0:T(8,128)(2,1)}) fusion(bf16[1280,640]{1,0:T(8,128)(2,1)S(1)} %copy-done.9, f32[256,2560]{1,0:T(8,128)S(1)} %fusion.198, f32[128,640]{1,0:T(8,128)S(1)} %copy-done.3, f32[640]{0:T(1024)S(1)} %convolution_reduce_fusion.2, bf16[256,640]{1,0:T(8,128)(2,1)} %collective-permute-done.5, ...), kind=kOutput, calls=%fused_computation.139 | convolution fusion | flops 443678464 | bytes 5737985 | tf_op jit(solution)/shard_map/dot_general | solution.py:51
  107.9 3.1 %collective-permute-start.6 = (bf16[256,640]{1,0:T(8,128)(2,1)}, bf16[256,640]{1,0:T(8,128)(2,1)}, u32[]{:S(2)}, u32[]{:S(2)}) collective-permute-start(bf16[256,640]{1,0:T(8,128)(2,1)} %get-tuple-element.12), channel_id=1, source_target_pairs={{0,8},{8,16},{16,24},{1,9},{9,17},{17,25},{2,10},{10,18},{18,26},{... | collective-permute-start | bytes 983048 | tf_op jit(solution)/shard_map/ppermute | solution.py:13
  111.0 1.5 %collective-permute-start.7 = (bf16[256,640]{1,0:T(8,128)(2,1)}, bf16[256,640]{1,0:T(8,128)(2,1)}, u32[]{:S(2)}, u32[]{:S(2)}) collective-permute-start(bf16[256,640]{1,0:T(8,128)(2,1)} %get-tuple-element.12), channel_id=1, source_target_pairs={{8,0},{16,8},{24,16},{0,24},{9,1},{17,9},{25,17},{1,25},{10,2},{18... | collective-permute-start | bytes 983048 | tf_op jit(solution)/shard_map/ppermute | solution.py:19
  113.9 7.3 %all-gather.7 = f32[4,4,128]{2,1,0:T(4,128)S(1)} all-gather(f32[1,4,128]{2,1,0:T(4,128)S(1)} %select_bitcast_fusion.1), channel_id=4, replica_groups=mesh['sect'=4,'batch'=8] {'sect'}, dimensions={0}, use_global_device_ids=true | all-gather | bytes 10240 | tf_op jit(solution)/shard_map/all_gather | solution.py:24
  122.8 2.4 %fusion.199 = f32[256,2560]{1,0:T(8,128)S(1)} fusion(bf16[640,2560]{1,0:T(8,128)(2,1)S(1)} %copy-done, f32[256]{0:T(256)S(1)} %add_rsqrt_fusion.1, f32[128,640]{1,0:T(8,128)S(1)} %copy-done.4, bf16[256,640]{1,0:T(8,128)(2,1)} %collective-permute-done.7, bf16[256,640]{1,0:T(8,128)(2,1)} %collective-permute-done.6, ...), kind=kOutput, calls=%fused_computation.268 | convolution fusion | flops 840990720 | bytes 7048705 | tf_op jit(solution)/shard_map/dot_general | solution.py:47
  125.2 4.6 %fusion.75 = (f32[256]{0:T(256)S(1)}, bf16[256,640]{1,0:T(8,128)(2,1)S(1)}) fusion(bf16[1280,640]{1,0:T(8,128)(2,1)S(1)} %copy-done.10, f32[256,2560]{1,0:T(8,128)S(1)} %fusion.199, f32[128,640]{1,0:T(8,128)S(1)} %copy-done.4, f32[640]{0:T(1024)S(1)} %convolution_reduce_fusion.1, bf16[256,640]{1,0:T(8,128)(2,1)} %collective-permute-done.7, ...), kind=kOutput, calls=%fused_computation.140 | convolution fusion | flops 443678464 | bytes 5737985 | tf_op jit(solution)/shard_map/dot_general | solution.py:51
  130.6 6.7 %all-gather.8 = f32[4,4,128]{2,1,0:T(4,128)S(1)} all-gather(f32[1,4,128]{2,1,0:T(4,128)S(1)} %select_bitcast_fusion), channel_id=5, replica_groups=mesh['sect'=4,'batch'=8] {'sect'}, dimensions={0}, use_global_device_ids=true | all-gather | bytes 10240 | tf_op jit(solution)/shard_map/all_gather | solution.py:24
  (82 shorter events, 10.5 us)
Async XLA Ops:
  7.2 48.0 %copy-start = (bf16[640,2560]{1,0:T(8,128)(2,1)S(1)}, bf16[640,2560]{1,0:T(8,128)(2,1)}, u32[]{:S(2)}) copy-start(bf16[640,2560]{1,0:T(8,128)(2,1)} %param.15) | copy-start | bytes 9830404
  7.2 51.8 %all-gather.11.cloned.1.call-start = ((), (), s32[]{:S(2)}) async-start(), calls=%async_computation | async-start | bytes 1843200 | tf_op jit(solution)/shard_map/all_gather | solution.py:63
  7.9 45.8 %collective-permute-start = (bf16[256,640]{1,0:T(8,128)(2,1)}, bf16[256,640]{1,0:T(8,128)(2,1)}, u32[]{:S(2)}, u32[]{:S(2)}) collective-permute-start(bf16[256,640]{1,0:T(8,128)(2,1)} %param.10), channel_id=1, source_target_pairs={{0,8},{8,16},{16,24},{1,9},{9,17},{17,25},{2,10},{10,18},{18,26},{... | collective-permute-start | bytes 983048 | tf_op jit(solution)/shard_map/ppermute | solution.py:13
  11.1 42.6 %collective-permute-start.1 = (bf16[256,640]{1,0:T(8,128)(2,1)}, bf16[256,640]{1,0:T(8,128)(2,1)}, u32[]{:S(2)}, u32[]{:S(2)}) collective-permute-start(bf16[256,640]{1,0:T(8,128)(2,1)} %param.10), channel_id=1, source_target_pairs={{8,0},{16,8},{24,16},{0,24},{9,1},{17,9},{25,17},{1,25},{10,2},{18... | collective-permute-start | bytes 983048 | tf_op jit(solution)/shard_map/ppermute | solution.py:19
  18.7 34.1 %copy-start.5 = (bf16[640,640]{1,0:T(8,128)(2,1)S(1)}, bf16[640,640]{1,0:T(8,128)(2,1)}, u32[]{:S(2)}) copy-start(bf16[640,640]{1,0:T(8,128)(2,1)} %param.16) | copy-start | bytes 2457604
  51.4 2.1 %copy-start.6 = (bf16[4,640]{1,0:T(4,128)(2,1)S(1)}, bf16[4,640]{1,0:T(4,128)(2,1)}, u32[]{:S(2)}) copy-start(bf16[4,640]{1,0:T(4,128)(2,1)} %param.18) | copy-start | bytes 15364
  51.4 2.1 %copy-start.7 = (f32[4,128]{1,0:T(4,128)S(1)}, f32[4,128]{1,0:T(4,128)}, u32[]{:S(2)}) copy-start(f32[4,128]{1,0:T(4,128)} %param.11) | copy-start | bytes 6148
  53.8 1.4 copy-start.1
  59.0 8.4 %copy-start.11 = (bf16[4,640]{1,0:T(4,128)(2,1)S(1)}, bf16[4,640]{1,0:T(4,128)(2,1)}, u32[]{:S(2)}) copy-start(bf16[4,640]{1,0:T(4,128)(2,1)} %param.19) | copy-start | bytes 15364
  65.4 13.1 %collective-permute-start.2 = (bf16[256,640]{1,0:T(8,128)(2,1)}, bf16[256,640]{1,0:T(8,128)(2,1)}, u32[]{:S(2)}, u32[]{:S(2)}) collective-permute-start(bf16[256,640]{1,0:T(8,128)(2,1)} %get-tuple-element.8), channel_id=1, source_target_pairs={{0,8},{8,16},{16,24},{1,9},{9,17},{17,25},{2,10},{10,18},{18,26},{... | collective-permute-start | bytes 983048 | tf_op jit(solution)/shard_map/ppermute | solution.py:13
  67.4 11.1 %collective-permute-start.3 = (bf16[256,640]{1,0:T(8,128)(2,1)}, bf16[256,640]{1,0:T(8,128)(2,1)}, u32[]{:S(2)}, u32[]{:S(2)}) collective-permute-start(bf16[256,640]{1,0:T(8,128)(2,1)} %get-tuple-element.8), channel_id=1, source_target_pairs={{8,0},{16,8},{24,16},{0,24},{9,1},{17,9},{25,17},{1,25},{10,2},{18... | collective-permute-start | bytes 983048 | tf_op jit(solution)/shard_map/ppermute | solution.py:19
  78.2 1.6 %copy-start.2 = (f32[128,640]{1,0:T(8,128)S(1)}, f32[128,640]{1,0:T(8,128)}, u32[]{:S(2)}) copy-start(f32[128,640]{1,0:T(8,128)} %copy-done.1) | copy-start | bytes 983044
  79.9 2.4 %copy-start.8 = (bf16[1280,640]{1,0:T(8,128)(2,1)S(1)}, bf16[1280,640]{1,0:T(8,128)(2,1)}, u32[]{:S(2)}) copy-start(bf16[1280,640]{1,0:T(8,128)(2,1)} %all-gather.11.cloned.1.call-done) | copy-start | bytes 4915204
  87.5 11.4 %collective-permute-start.4 = (bf16[256,640]{1,0:T(8,128)(2,1)}, bf16[256,640]{1,0:T(8,128)(2,1)}, u32[]{:S(2)}, u32[]{:S(2)}) collective-permute-start(bf16[256,640]{1,0:T(8,128)(2,1)} %get-tuple-element.10), channel_id=1, source_target_pairs={{0,8},{8,16},{16,24},{1,9},{9,17},{17,25},{2,10},{10,18},{18,26},{... | collective-permute-start | bytes 983048 | tf_op jit(solution)/shard_map/ppermute | solution.py:13
  90.7 8.2 %collective-permute-start.5 = (bf16[256,640]{1,0:T(8,128)(2,1)}, bf16[256,640]{1,0:T(8,128)(2,1)}, u32[]{:S(2)}, u32[]{:S(2)}) collective-permute-start(bf16[256,640]{1,0:T(8,128)(2,1)} %get-tuple-element.10), channel_id=1, source_target_pairs={{8,0},{16,8},{24,16},{0,24},{9,1},{17,9},{25,17},{1,25},{10,2},{18... | collective-permute-start | bytes 983048 | tf_op jit(solution)/shard_map/ppermute | solution.py:19
  98.7 1.6 %copy-start.3 = (f32[128,640]{1,0:T(8,128)S(1)}, f32[128,640]{1,0:T(8,128)}, u32[]{:S(2)}) copy-start(f32[128,640]{1,0:T(8,128)} %copy-done.1) | copy-start | bytes 983044
  100.3 2.4 %copy-start.9 = (bf16[1280,640]{1,0:T(8,128)(2,1)S(1)}, bf16[1280,640]{1,0:T(8,128)(2,1)}, u32[]{:S(2)}) copy-start(bf16[1280,640]{1,0:T(8,128)(2,1)} %all-gather.11.cloned.1.call-done) | copy-start | bytes 4915204
  107.9 13.5 %collective-permute-start.6 = (bf16[256,640]{1,0:T(8,128)(2,1)}, bf16[256,640]{1,0:T(8,128)(2,1)}, u32[]{:S(2)}, u32[]{:S(2)}) collective-permute-start(bf16[256,640]{1,0:T(8,128)(2,1)} %get-tuple-element.12), channel_id=1, source_target_pairs={{0,8},{8,16},{16,24},{1,9},{9,17},{17,25},{2,10},{10,18},{18,26},{... | collective-permute-start | bytes 983048 | tf_op jit(solution)/shard_map/ppermute | solution.py:13
  111.0 10.4 %collective-permute-start.7 = (bf16[256,640]{1,0:T(8,128)(2,1)}, bf16[256,640]{1,0:T(8,128)(2,1)}, u32[]{:S(2)}, u32[]{:S(2)}) collective-permute-start(bf16[256,640]{1,0:T(8,128)(2,1)} %get-tuple-element.12), channel_id=1, source_target_pairs={{8,0},{16,8},{24,16},{0,24},{9,1},{17,9},{25,17},{1,25},{10,2},{18... | collective-permute-start | bytes 983048 | tf_op jit(solution)/shard_map/ppermute | solution.py:19
  121.2 1.6 %copy-start.4 = (f32[128,640]{1,0:T(8,128)S(1)}, f32[128,640]{1,0:T(8,128)}, u32[]{:S(2)}) copy-start(f32[128,640]{1,0:T(8,128)} %copy-done.1) | copy-start | bytes 983044
  122.8 2.4 %copy-start.10 = (bf16[1280,640]{1,0:T(8,128)(2,1)S(1)}, bf16[1280,640]{1,0:T(8,128)(2,1)}, u32[]{:S(2)}) copy-start(bf16[1280,640]{1,0:T(8,128)(2,1)} %all-gather.11.cloned.1.call-done) | copy-start | bytes 4915204
  129.9 0.7 copy-start.12
Sparse Core Ops, SparseCore 0:
  10.2 47.5 all-gather.10
